TPU v7x, 256 devices: a whole 4x4x8 slice. The times are simulated.
256 devices in a mesh: seq: 32 (over x, z), head: 8 (over y, core).
Axes of the slice: x: 4, y: 4, z: 8, core: 2. Of those that a mesh axis runs over, the one named last changes fastest.
Arguments:
- cached_probs: bfloat16 [128, 40, 8, 128, 128], P('seq', 'head'), may hold values from 0 to 1, as said below
- out_old: bfloat16 [16384, 5120], P('seq', 'head'), may hold values from -6 to 6
- key_lists: int32 [128, 8], P('seq'), may hold values from 0 to 127, as said below
- changed_block_numbers: int32 [32], replicated, may hold values from 0 to 127, as said below
- delta_v: bfloat16 [4096, 1024], P('seq', 'head'), may hold values from -24 to 24
- w_out: bfloat16 [5120, 5120], P('head', 'seq'), may hold values from -0.078125 to 0.078125
Outputs:
- attn_new: bfloat16 [16384, 5120], P('seq', 'head')
- out_proj: bfloat16 [16384, 5120], P('seq', 'head')
Inputs may be any that keep to these rules, and one draw needn't show every extreme that they name: `changed_block_numbers`: the changed block numbers are all different; the first block and the last block are always among them. `key_lists`: each query block lists 8 different key blocks; some list many changed blocks, most list few. `cached_probs`: for each query block, head and row, the weights over the row's listed keys are positive and sum to at most 1.
All inputs are finite; a program needn't handle non-finite values.
Results may differ from a plain program's by a relative error of at most 0.017.
Values may be sent and summed in bfloat16 or wider, within the bound.
A program may use at most 128 MiB of HBM per device.

v0:
```python
import jax
import jax.numpy as jnp
from jax import lax
from jax.sharding import PartitionSpec as P

HD = 128
BLK = 128
GROUP = 5


def local(cached_probs, out_old, key_lists, changed_block_numbers, delta_v, w_out):
    blocks_here = cached_probs.shape[0]
    heads_here = cached_probs.shape[1]
    topk_here = cached_probs.shape[2]
    values_here = heads_here // GROUP
    change_rows = delta_v.reshape(delta_v.shape[0] // BLK, BLK * values_here * HD)
    flat_lists = key_lists.reshape(blocks_here * topk_here)
    every_change = lax.all_gather(change_rows, "seq", axis=0, tiled=True)
    onehot = (flat_lists[:, None] == changed_block_numbers[None, :]).astype(jnp.bfloat16)
    selected = jnp.dot(onehot, every_change, preferred_element_type=jnp.float32)
    picked = selected.astype(jnp.bfloat16).reshape(blocks_here, topk_here, BLK, values_here, HD)
    tiles = cached_probs.reshape(blocks_here, values_here, GROUP, topk_here, BLK, BLK)
    delta_out = jnp.einsum("qvgkij,qkjvd->qivgd", tiles, picked, preferred_element_type=jnp.float32)
    delta_out = delta_out.reshape(blocks_here * BLK, heads_here * HD)
    attn_new = (out_old.astype(jnp.float32) + delta_out).astype(jnp.bfloat16)
    terms = jnp.dot(
        attn_new,
        lax.all_gather(w_out, "seq", axis=1, tiled=True),
        preferred_element_type=jnp.float32,
    )
    out_proj = lax.psum_scatter(terms.astype(jnp.bfloat16), "head", scatter_dimension=1, tiled=True)
    return (attn_new, out_proj)


def solution(mesh):
    placed = (
        P("seq", "head", None, None, None),
        P("seq", "head"),
        P("seq", None),
        P(),
        P("seq", "head"),
        P("head", "seq"),
    )
    return jax.shard_map(
        local,
        mesh=mesh,
        in_specs=placed,
        out_specs=(P("seq", "head"), P("seq", "head")),
        check_vma=False,
    )
```

profile of v0, /device:TPU:2, one launch (start us, length us, event | category | flops | bytes accessed | tf_op | source)
XLA Modules:
  0.0 247.0 jit_solution(4615410390081621917)
XLA Ops:
  7.2 0.0 all-gather.6.cloned.1.call-start
  7.2 1.4 reshape.24
  8.6 0.0 all-gather.6.cloned.1.call-update
  8.6 0.0 all-gather.4.cloned.1.call-start
  8.7 0.7 all-gather.4.cloned.1.call-update
  9.4 0.0 copy-start.1
  9.4 0.0 copy-start
  9.4 0.0 copy-start.2
  9.4 0.0 reduce-scatter.4.cloned.1.call-start
  9.5 8.7 %copy.14 = bf16[4,5,8,128,128]{3,2,4,1,0:T(8,128)(2,1)} copy(bf16[4,5,8,128,128]{4,3,2,1,0:T(8,128)(2,1)} %param.6) | data formatting | bytes 10485760 | tf_op args[0]
  18.1 0.0 copy-done.1
  18.1 0.1 eq.15
  18.2 0.0 copy-done
  18.2 0.3 copy.13
  18.5 72.4 %all-gather.6.cloned.1.call-done = bf16[32,1,16384]{2,1,0:T(2,128)(2,1)} async-done(((bf16[1,1,16384]{2,1,0:T(2,128)(2,1)}), bf16[32,1,16384]{2,1,0:T(2,128)(2,1)}) %all-gather.6.cloned.1.call-update) | async-done | bytes 1048592 | tf_op jit(solution)/shard_map/all_gather | solution.py:18
  90.9 0.0 copy-done.2
  90.9 5.3 %convolution_bitcast_fusion = f32[4,128,1,5,128]{1,4,3,0,2:T(8,128)S(1)} fusion(bf16[4,5,8,128,128]{3,2,4,1,0:T(8,128)(2,1)} %copy.14, bf16[32,1,16384]{2,1,0:T(2,128)(2,1)} %all-gather.6.cloned.1.call-done, s32[32]{0:T(128)S(1)} %copy-done.2, s32[32]{0:T(128)S(1)} %eq.15), kind=kOutput, calls=%fused_computation.2 | convolution fusion | flops 705168384 | bytes 7602432 | tf_op jit(solution)/shard_map/qvgkij,qkjvd->qivgd/dot_general | solution.py:23
  96.2 0.8 copy.15
  97.1 0.3 fusion.1
  97.3 83.0 %all-gather.4.cloned.1.call-done = bf16[640,5120]{0,1:T(8,128)(2,1)} async-done(((bf16[640,160]{0,1:T(8,128)(2,1)}), bf16[640,5120]{0,1:T(8,128)(2,1)}) %all-gather.4.cloned.1.call-update) | async-done | bytes 6553616 | tf_op jit(solution)/shard_map/all_gather | solution.py:28
  180.3 8.9 %convolution_convert_fusion.1 = bf16[512,5120]{1,0:T(8,128)(2,1)} fusion(bf16[512,640]{0,1:T(8,128)(2,1)S(1)} %fusion.1, bf16[640,5120]{0,1:T(8,128)(2,1)} %all-gather.4.cloned.1.call-done), kind=kOutput, calls=%fused_computation.1 | convolution fusion | flops 3358064640 | bytes 12451840 | tf_op jit(solution)/shard_map/dot_general | solution.py:26
  189.3 7.9 %copy.19 = bf16[512,5120]{0,1:T(8,128)(2,1)} copy(bf16[512,5120]{1,0:T(8,128)(2,1)} %convolution_convert_fusion.1) | data formatting | bytes 10485760
  197.2 0.0 reduce-scatter.4.cloned.1.call-update
  197.2 1.1 copy.16
  198.3 40.0 %reduce-scatter.4.cloned.1.call-done = bf16[640,512]{1,0:T(8,128)(2,1)} async-done(((bf16[5120,512]{1,0:T(8,128)(2,1)}), bf16[640,512]{1,0:T(8,128)(2,1)}) %reduce-scatter.4.cloned.1.call-update) | async-done | bytes 655376
  238.3 2.2 copy.20
Async XLA Ops:
  7.2 83.7 %all-gather.6.cloned.1.call-start = ((), (), s32[]{:S(2)}) async-start(), calls=%async_computation.2 | async-start | bytes 2162688 | tf_op jit(solution)/shard_map/all_gather | solution.py:18
  8.6 171.7 %all-gather.4.cloned.1.call-start = ((), (), s32[]{:S(2)}) async-start(), calls=%async_computation.1 | async-start | bytes 6758400 | tf_op jit(solution)/shard_map/all_gather | solution.py:28
  9.4 8.7 %copy-start.1 = (s32[4,8]{1,0:T(4,128)S(1)}, s32[4,8]{1,0:T(4,128)}, u32[]{:S(2)}) copy-start(s32[4,8]{1,0:T(4,128)} %param.8) | copy-start | bytes 388
  9.4 8.8 %copy-start = (bf16[512,640]{1,0:T(8,128)(2,1)S(1)}, bf16[512,640]{1,0:T(8,128)(2,1)}, u32[]{:S(2)}) copy-start(bf16[512,640]{1,0:T(8,128)(2,1)} %param.7) | copy-start | bytes 1966084
  9.4 81.5 %copy-start.2 = (s32[32]{0:T(128)S(1)}, s32[32]{0:T(128)}, u32[]{:S(2)}) copy-start(s32[32]{0:T(128)} %param.9) | copy-start | bytes 388
  9.4 228.8 %reduce-scatter.4.cloned.1.call-start = ((), (), s32[]{:S(2)}) async-start(), calls=%async_computation.3 | async-start | bytes 5898240
Sparse Core Ops, SparseCore 0:
  11.2 79.6 all-gather.5
  93.5 86.8 all-gather.3
  197.3 40.8 reduce-scatter.3
where the time goes:
time: 248 us; the launch traced here: 247 us
  waiting for transfers between devices  196 us (79%)
  local copies, waits for them, and re-layouts  22.4 us (9%)
  matrix products  14.3 us (6%)
  between operations  13.8 us (6%)
    all_gather x1, waiting for transfers between devices, local(): lax.all_gather(w_out, 'seq', axis=1, tiled=True)  83 us
    all_gather x1, waiting for transfers between devices, local(): every_change = lax.all_gather(change_rows, 'seq', axis=0, tiled=True)  72.4 us
    unnamed x4, waiting for transfers between devices  40.7 us
    unnamed x12, local copies, waits for them, and re-layouts  21.5 us
    dot_general x1, matrix products, local(): jnp.dot(attn_new, lax.all_gather(w_out, 'seq', axis=1, tiled=True), prefe...  8.95 us
    dot_general x1, matrix products, local(): jnp.einsum('qvgkij,qkjvd->qivgd', tiles, picked, preferred_element_type=j...  5.33 us
  transfers between devices with their start and end apart: 3, of which 3 were waited for; matrix products, arithmetic and copies ran while one was open for 7% of the time, Pallas kernels for 0%

commit v1 on v0

--- a/solution.py
+++ b/solution.py
@@ -8,6 +8,11 @@
 GROUP = 5
 
 
+def tiled_gather(shard, axis, dim):
+    copies = jnp.concatenate([shard] * lax.axis_size(axis), axis=dim)
+    return lax.all_to_all(copies, axis, dim, dim, tiled=True)
+
+
 def local(cached_probs, out_old, key_lists, changed_block_numbers, delta_v, w_out):
     blocks_here = cached_probs.shape[0]
     heads_here = cached_probs.shape[1]
@@ -15,7 +20,7 @@
     values_here = heads_here // GROUP
     change_rows = delta_v.reshape(delta_v.shape[0] // BLK, BLK * values_here * HD)
     flat_lists = key_lists.reshape(blocks_here * topk_here)
-    every_change = lax.all_gather(change_rows, "seq", axis=0, tiled=True)
+    every_change = tiled_gather(change_rows, "seq", 0)
     onehot = (flat_lists[:, None] == changed_block_numbers[None, :]).astype(jnp.bfloat16)
     selected = jnp.dot(onehot, every_change, preferred_element_type=jnp.float32)
     picked = selected.astype(jnp.bfloat16).reshape(blocks_here, topk_here, BLK, values_here, HD)

time: 248 us -> 179 us (0.72)
  waiting for transfers between devices: 196 us -> 102 us
  starting transfers between devices: 0.12 us -> 11.9 us
  other arithmetic: 0.25 us -> 8.39 us
  local copies, waits for them, and re-layouts: 22.4 us -> 27.7 us
    all_gather x1 -> x0, waiting for transfers between devices: 72.4 us -> none  [local(): every_change = lax.all_gather(change_rows, 'seq', axis=0, tiled=True)]
    all_gather x1, waiting for transfers between devices: 83 us -> 39.7 us  [local(): lax.all_gather(w_out, 'seq', axis=1, tiled=True)]
    all_to_all x0 -> x1, waiting for transfers between devices: none -> 21.9 us  [tiled_gather(): return lax.all_to_all(copies, axis, dim, dim, tiled=True)]
    all_to_all x0 -> x1, starting transfers between devices: none -> 11.6 us  [tiled_gather(): return lax.all_to_all(copies, axis, dim, dim, tiled=True)]
    concatenate x0 -> x1, other arithmetic: none -> 7.05 us  [tiled_gather(): copies = jnp.concatenate([shard] * lax.axis_size(axis), axis=dim)]
    concatenate x0 -> x2, local copies, waits for them, and re-layouts: none -> 3.15 us  [tiled_gather(): copies = jnp.concatenate([shard] * lax.axis_size(axis), axis=dim)]
    unnamed x12 -> x13, local copies, waits for them, and re-layouts: 21.5 us -> 23.6 us
    unnamed x4 -> x3, waiting for transfers between devices: 40.7 us -> 40.7 us
  transfers between devices with their start and end apart: 3 -> 3, of which waited for: 3 -> 3; matrix products, arithmetic and copies ran while one was open for 7% -> 17% of each run, Pallas kernels for 0% -> 0%
where the time goes in v1:
time: 179 us; the launch traced here: 178 us
  waiting for transfers between devices  102 us (57%)
  local copies, waits for them, and re-layouts  27.7 us (15%)
  between operations  14.1 us (8%)
  matrix products  13.6 us (8%)
  starting transfers between devices  11.9 us (7%)
  other arithmetic  8.39 us (5%)
    unnamed x3, waiting for transfers between devices  40.7 us
    all_gather x1, waiting for transfers between devices, local(): lax.all_gather(w_out, 'seq', axis=1, tiled=True)  39.7 us
    unnamed x13, local copies, waits for them, and re-layouts  23.6 us
    all_to_all x1, waiting for transfers between devices, tiled_gather(): return lax.all_to_all(copies, axis, dim, dim, tiled=True)  21.9 us
    all_to_all x1, starting transfers between devices, tiled_gather(): return lax.all_to_all(copies, axis, dim, dim, tiled=True)  11.6 us
    dot_general x1, matrix products, local(): jnp.dot(attn_new, lax.all_gather(w_out, 'seq', axis=1, tiled=True), prefe...  8.93 us
    concatenate x1, other arithmetic, tiled_gather(): copies = jnp.concatenate([shard] * lax.axis_size(axis), axis=dim)  7.05 us
    dot_general x1, matrix products, local(): jnp.einsum('qvgkij,qkjvd->qivgd', tiles, picked, preferred_element_type=j...  4.69 us
  transfers between devices with their start and end apart: 3, of which 3 were waited for; matrix products, arithmetic and copies ran while one was open for 17% of the time, Pallas kernels for 0%

profile of v1, /device:TPU:2, one launch (start us, length us, event | category | flops | bytes accessed | tf_op | source)
XLA Modules:
  0.0 177.9 jit_solution(17733729967381737898)
XLA Ops:
  7.2 0.0 all-gather.2.cloned.1.call-start
  7.2 0.7 all-gather.2.cloned.1.call-update
  7.9 2.6 %concatenate.6 = bf16[32,1,16384]{2,1,0:T(2,128)(2,1)S(1)} broadcast(bf16[16384]{0:T(1024)(128)(2,1)} %bitcast.36), dimensions={2} | broadcast | bytes 1081344 | tf_op jit(solution)/shard_map/concatenate | solution.py:12
  10.5 0.5 broadcast.5
  11.1 7.1 %reduce = bf16[32,16384]{1,0:T(8,128)(2,1)S(1)} reduce(bf16[32,1,16384]{2,1,0:T(2,128)(2,1)S(1)} %concatenate.6, bf16[]{:T(256)} %broadcast.5), dimensions={1}, to_apply=%concatenate.6.reduce_sub_computation | reduce | bytes 2097154 | tf_op jit(solution)/shard_map/concatenate | solution.py:12
  18.1 1.6 reshape.34
  19.7 11.6 %all-to-all-start = ((bf16[32,2,8192]{2,1,0:T(2,128)(2,1)}), bf16[32,2,8192]{2,1,0:T(2,128)(2,1)S(1)}, u32[]{:S(2)}, u32[]{:S(2)}) async-start(bf16[32,2,8192]{2,1,0:T(2,128)(2,1)} %reshape.34), calls=%async_computation | async-start | bytes 2097152 | tf_op jit(solution)/shard_map/all_to_all | solution.py:13
  31.4 0.0 copy-start.1
  31.4 0.0 copy-start
  31.4 0.0 copy-start.2
  31.4 0.2 reduce-scatter.4.cloned.1.call-start
  31.6 8.7 %copy.14 = bf16[4,5,8,128,128]{3,2,4,1,0:T(8,128)(2,1)} copy(bf16[4,5,8,128,128]{4,3,2,1,0:T(8,128)(2,1)} %param.6) | data formatting | bytes 10485760 | tf_op args[0]
  40.3 0.0 copy-done.1
  40.3 0.1 eq.15
  40.4 0.0 copy-done
  40.4 1.1 copy.13
  41.5 21.9 %all-to-all-done = bf16[32,2,8192]{2,1,0:T(2,128)(2,1)S(1)} async-done(((bf16[32,2,8192]{2,1,0:T(2,128)(2,1)}), bf16[32,2,8192]{2,1,0:T(2,128)(2,1)S(1)}, u32[]{:S(2)}, u32[]{:S(2)}) %all-to-all-start) | async-done | bytes 1048608 | tf_op jit(solution)/shard_map/all_to_all | solution.py:13
  63.3 1.0 reshape.35
  64.4 0.0 copy-done.2
  64.4 4.7 %convolution_bitcast_fusion = f32[4,128,1,5,128]{1,4,3,0,2:T(8,128)S(1)} fusion(bf16[4,5,8,128,128]{3,2,4,1,0:T(8,128)(2,1)} %copy.14, bf16[32,1,16384]{2,1,0:T(2,128)(2,1)S(1)} %reshape.35, s32[32]{0:T(128)S(1)} %copy-done.2, s32[32]{0:T(128)S(1)} %eq.15), kind=kOutput, calls=%fused_computation.2 | convolution fusion | flops 705168384 | bytes 7602432 | tf_op jit(solution)/shard_map/qvgkij,qkjvd->qivgd/dot_general | solution.py:28
  69.1 0.8 copy.15
  69.9 1.3 fusion.1
  71.3 39.7 %all-gather.2.cloned.1.call-done = bf16[640,5120]{0,1:T(8,128)(2,1)} async-done(((bf16[640,160]{0,1:T(8,128)(2,1)}), bf16[640,5120]{0,1:T(8,128)(2,1)}) %all-gather.2.cloned.1.call-update) | async-done | bytes 6553616 | tf_op jit(solution)/shard_map/all_gather | solution.py:33
  111.0 8.9 %convolution_convert_fusion.1 = bf16[512,5120]{1,0:T(8,128)(2,1)} fusion(bf16[512,640]{0,1:T(8,128)(2,1)S(1)} %fusion.1, bf16[640,5120]{0,1:T(8,128)(2,1)} %all-gather.2.cloned.1.call-done), kind=kOutput, calls=%fused_computation.1 | convolution fusion | flops 3358064640 | bytes 12451840 | tf_op jit(solution)/shard_map/dot_general | solution.py:31
  119.9 7.9 %copy.19 = bf16[512,5120]{0,1:T(8,128)(2,1)} copy(bf16[512,5120]{1,0:T(8,128)(2,1)} %convolution_convert_fusion.1) | data formatting | bytes 10485760
  127.9 0.0 reduce-scatter.4.cloned.1.call-update
  127.9 1.1 copy.16
  129.0 40.0 %reduce-scatter.4.cloned.1.call-done = bf16[640,512]{1,0:T(8,128)(2,1)} async-done(((bf16[5120,512]{1,0:T(8,128)(2,1)}), bf16[640,512]{1,0:T(8,128)(2,1)}) %reduce-scatter.4.cloned.1.call-update) | async-done | bytes 655376
  168.9 2.2 %copy.20 = bf16[512,640]{1,0:T(8,128)(2,1)} copy(bf16[512,640]{0,1:T(8,128)(2,1)} %bitcast.35) | data formatting | bytes 1310720
Async XLA Ops:
  7.2 103.8 %all-gather.2.cloned.1.call-start = ((), (), s32[]{:S(2)}) async-start(), calls=%async_computation.2 | async-start | bytes 6758400 | tf_op jit(solution)/shard_map/all_gather | solution.py:33
  19.7 43.6 %all-to-all-start = ((bf16[32,2,8192]{2,1,0:T(2,128)(2,1)}), bf16[32,2,8192]{2,1,0:T(2,128)(2,1)S(1)}, u32[]{:S(2)}, u32[]{:S(2)}) async-start(bf16[32,2,8192]{2,1,0:T(2,128)(2,1)} %reshape.34), calls=%async_computation | async-start | bytes 2097152 | tf_op jit(solution)/shard_map/all_to_all | solution.py:13
  31.4 8.9 %copy-start.1 = (s32[4,8]{1,0:T(4,128)S(1)}, s32[4,8]{1,0:T(4,128)}, u32[]{:S(2)}) copy-start(s32[4,8]{1,0:T(4,128)} %param.8) | copy-start | bytes 388
  31.4 9.0 %copy-start = (bf16[512,640]{1,0:T(8,128)(2,1)S(1)}, bf16[512,640]{1,0:T(8,128)(2,1)}, u32[]{:S(2)}) copy-start(bf16[512,640]{1,0:T(8,128)(2,1)} %param.7) | copy-start | bytes 1966084
  31.4 33.0 %copy-start.2 = (s32[32]{0:T(128)S(1)}, s32[32]{0:T(128)}, u32[]{:S(2)}) copy-start(s32[32]{0:T(128)} %param.9) | copy-start | bytes 388
  31.4 137.5 %reduce-scatter.4.cloned.1.call-start = ((), (), s32[]{:S(2)}) async-start(), calls=%async_computation.3 | async-start | bytes 5898240
Sparse Core Ops, SparseCore 0:
  10.6 100.3 all-gather.1
  128.0 40.8 reduce-scatter.3
